TPU v7x, 32 devices: a whole 2x2x4 slice. The times are simulated.
32 devices in a mesh: dp: 4 (over y, core), owner: 8 (over z, x).
Axes of the slice: x: 2, y: 2, z: 4, core: 2. Of those that a mesh axis runs over, the one named last changes fastest.
Arguments:
- embeddings: bfloat16 [131072, 1024], P(('dp', 'owner')), may hold values from -40 to 40, as said below
- cluster_ids: int32 [131072, 1], P(('dp', 'owner')), may hold values from 0 to 63; in each aligned block of 4096 rows (0 to 4095, 4096 to 8191, ...) at most 128 rows name the same one
- noise: bfloat16 [131072, 256], P(('dp', 'owner')), may hold values from -3 to 3
- start_basis: float32 [1024, 256], replicated, may hold values from -0.1875 to 0.1875
Outputs:
- routed: bfloat16 [4, 64, 8, 128, 256], P('dp', 'owner')
Inputs may be any that keep to these rules, and one draw needn't show every extreme that they name: `embeddings`: entries are of order one around a column mean. `cluster_ids`: no cluster holds more than 128 rows of one device, and some cluster holds exactly 128 rows of some device.
All inputs are finite; a program needn't handle non-finite values.
Results may differ from a plain program's by a relative error of at most 0.0046.
Values may be sent and summed in bfloat16 or wider, within the bound.
No kernel may reach another device: no remote copies, remote signals or barrier semaphores. Data moves between devices by JAX's collectives and lax.ppermute only.
A program may use at most 128 MiB of HBM per device.

v0:
```python
import math
import jax
import jax.numpy as jnp
from jax import lax
from jax.sharding import PartitionSpec as P

CL_DEV = 8


def shards(embeddings, cluster_ids, noise, start_basis):
    highest = lax.Precision.HIGHEST
    rows_dev, feature_width = embeddings.shape
    rank_count = start_basis.shape[1]
    owners = lax.axis_size("owner")
    row_total = rows_dev * lax.axis_size("dp") * owners
    column_sum = jnp.sum(embeddings, axis=0, dtype=jnp.float32)
    second = lax.dot_general(
        embeddings, embeddings, (((0,), (0,)), ((), ())), preferred_element_type=jnp.float32
    )
    second_all, column_all = lax.psum((second, column_sum), ("dp", "owner"))
    mean_vec = column_all / row_total
    covariance = second_all / row_total - jnp.outer(mean_vec, mean_vec)
    image_rows = jnp.dot(covariance, start_basis, precision=highest)
    gram_matrix = jnp.dot(image_rows.T, image_rows, precision=highest)
    lower_factor = jnp.linalg.cholesky(gram_matrix)
    basis_full = lax.linalg.triangular_solve(
        lower_factor, image_rows, left_side=False, lower=True, transpose_a=True
    )
    curved = jnp.dot(covariance, basis_full, precision=highest)
    eigen_vals = jnp.sum(basis_full * curved, axis=0)
    signed = math.sqrt(feature_width) * jnp.sum(basis_full, axis=0)
    flip_sign = signed / jnp.maximum(jnp.abs(signed), 1.0)
    whiten = (basis_full * (flip_sign / jnp.sqrt(eigen_vals + 1e-06))).astype(jnp.bfloat16)
    offset = jnp.dot(mean_vec, whiten.astype(jnp.float32), precision=highest)
    clusters = CL_DEV * owners
    capacity = 2 * rows_dev // clusters
    ids_here = cluster_ids[:, 0]
    onehot = (cluster_ids == jnp.arange(clusters, dtype=jnp.int32)[None, :]).astype(jnp.int32)
    before = jnp.cumsum(onehot, axis=0) - onehot
    slot_index = jnp.sum(before * onehot, axis=1)
    destination = ids_here * capacity + slot_index
    projected = (
        jnp.dot(embeddings, whiten, preferred_element_type=jnp.float32)
        - offset
        + noise.astype(jnp.float32)
    ).astype(jnp.bfloat16)
    packed = (
        jnp.zeros((clusters * capacity, rank_count), jnp.bfloat16).at[destination].set(projected)
    )
    packed = packed.reshape(clusters, 1, capacity, rank_count)
    arrived = lax.all_to_all(packed, "owner", split_axis=0, concat_axis=1, tiled=True)
    return arrived[None]


def solution(mesh):
    return jax.shard_map(
        shards,
        mesh=mesh,
        in_specs=(
            P(("dp", "owner"), None),
            P(("dp", "owner"), None),
            P(("dp", "owner"), None),
            P(),
        ),
        out_specs=P("dp", "owner", None, None, None),
        check_vma=False,
    )
```

profile of v0, /device:TPU:0, one launch (start us, length us, event | category | flops | bytes accessed | tf_op | source)
XLA Modules:
  0.0 376.8 jit_solution(5720101799312781308)
XLA Ops:
  6.5 0.0 copy-start
  6.5 0.0 all-reduce.3.cloned.1.call-start
  6.5 15.1 %fusion.32 = f32[1024,1024]{1,0:T(8,128)} fusion(bf16[4096,1024]{1,0:T(8,128)(2,1)} %param.4), kind=kOutput, calls=%fused_computation.64 | convolution fusion | flops 8589934592 | bytes 12582912 | tf_op jit(solution)/shard_map/dot_general | solution.py:17
  21.6 0.0 all-reduce.3.cloned.1.call-update
  21.7 1.6 copy-done.2
  23.2 2.9 copy.20
  26.1 0.0 copy-done.4
  26.1 0.1 fusion.18
  26.3 18.4 %reduce-window.6 = s32[64,32,128]{2,1,0:T(8,128)S(1)} reduce-window(s32[64,32,128]{2,1,0:T(8,128)S(1)} %fusion.18, s32[]{:T(128)} %copy.38), window={size=1x1x128 pad=0_0x0_0x127_0}, to_apply=%region_0.0 | reduce-window | flops 33292288 | bytes 2097156 | tf_op jit(solution)/shard_map/reduce-window
  44.7 0.3 slice.61
  45.1 0.4 copy.25
  45.5 0.2 reduce-window.9
  45.7 4.7 %convert_reduce_fusion = f32[1024]{0:T(1024)S(1)} fusion(bf16[4096,1024]{1,0:T(8,128)(2,1)} %param.4), kind=kLoop, calls=%fused_computation.3 | loop fusion | flops 8387584 | bytes 8392704 | tf_op jit(solution)/shard_map/reduce_sum | solution.py:16
  50.4 42.3 %psum.15 = f32[1024]{0:T(1024)S(1)} all-reduce(f32[1024]{0:T(1024)S(1)} %convert_reduce_fusion), channel_id=1, replica_groups=mesh['dp'=4,'owner'=8] {'dp','owner'}, use_global_device_ids=true, to_apply=%region_5.6 | all-reduce | flops 1024 | bytes 8192 | tf_op jit(solution)/shard_map/psum | solution.py:20
  92.7 0.3 broadcast_add_fusion
  93.0 0.9 fusion.17
  94.0 73.1 %all-reduce.3.cloned.1.call-done = f32[1024,1024]{1,0:T(8,128)} async-done(((f32[1024,1024]{1,0:T(8,128)}), f32[1024,1024]{1,0:T(8,128)}) %all-reduce.3.cloned.1.call-update) | async-done | bytes 4194320 | tf_op jit(solution)/shard_map/psum | solution.py:20
  167.1 0.0 copy-done
  167.1 6.1 %fusion.4 = f32[1024,256]{1,0:T(8,128)S(1)} fusion(f32[1024,256]{1,0:T(8,128)S(1)} %copy-done, f32[1024,1024]{1,0:T(8,128)} %all-reduce.3.cloned.1.call-done, f32[1024]{0:T(1024)S(1)} %broadcast_multiply_fusion), kind=kOutput, calls=%fused_computation.10 | convolution fusion | flops 3224371200 | bytes 6295552 | tf_op jit(solution)/shard_map/dot_general | solution.py:23
  173.2 1.8 fusion.33
  175.0 0.1 copy.18
  175.2 11.7 %cholesky.50 = f32[128,128]{1,0:T(8,128)S(1)} custom-call(f32[128,128]{1,0:T(8,128)S(1)} %cholesky.118), custom_call_target="Cholesky" | custom-call | tf_op jit(solution)/shard_map/jit(cholesky)/cholesky | solution.py:25
  187.0 9.8 %custom-call.14 = f32[1,128,128]{1,2,0:T(8,128)S(1)} custom-call(f32[1,128,128]{2,1,0:T(8,128)S(1)} %get-tuple-element.26), custom_call_target="InvertDiagBlocksLowerTriangular" | custom-call | tf_op jit(solution)/shard_map/jit(cholesky)/cholesky | solution.py:25
  196.8 0.2 constant_dynamic-update-slice_fusion.1
  197.0 0.3 convolution_subtract_fusion.2
  197.3 11.7 %cholesky.105 = f32[128,128]{1,0:T(8,128)S(1)} custom-call(f32[128,128]{1,0:T(8,128)S(1)} %convolution_subtract_fusion.2), custom_call_target="Cholesky" | custom-call | tf_op jit(solution)/shard_map/jit(cholesky)/cholesky | solution.py:25
  209.0 0.7 compare_reduce_fusion
  211.2 0.1 triangular_solve.58
  211.3 4.0 %while.1 = (s32[]{:T(128)}, f32[256,256]{1,0:T(8,128)S(1)}, s32[2,2]{1,0:T(2,128)S(1)}, f32[2,128,128]{2,1,0:T(8,128)S(1)}, s32[]{:T(128)}) while((s32[]{:T(128)}, f32[256,256]{1,0:T(8,128)S(1)}, s32[2,2]{1,0:T(2,128)S(1)}, f32[2,128,128]{2,1,0:T(8,128)S(1)}, s32[]{:T(128)}) %tuple.23), condition=%wide.while_cond, body=%wide.while_body.sunk | while | flops 2 | bytes 131181 | solution.py:26
  211.3 0.6 fusion.49
  211.9 1.4 bitcast_dynamic-update-slice_fusion.2
  213.3 0.6 fusion.49
  213.9 1.4 bitcast_dynamic-update-slice_fusion.2
  215.3 19.7 %custom-call.15 = f32[2,128,128]{1,2,0:T(8,128)S(1)} custom-call(f32[2,128,128]{2,1,0:T(8,128)S(1)} %get-tuple-element.12), custom_call_target="InvertDiagBlocksLowerTriangular" | custom-call | tf_op jit(solution)/shard_map/triangular_solve | solution.py:26
  234.9 0.0 copy-start.1
  235.0 0.6 fusion.20
  235.6 1.0 convolution_subtract_fusion.1
  236.6 0.6 fusion.23
  237.2 0.2 fusion.19
  237.4 0.0 copy-done.1
  237.4 4.5 %fusion.14 = f32[256]{0:T(256)S(1)} fusion(f32[1024,1024]{1,0:T(8,128)S(1)} %copy-done.1, f32[1024]{0:T(1024)S(1)} %broadcast_multiply_fusion, f32[1024,128]{0,1:T(8,128)S(1)} %fusion.23, f32[1024,128]{0,1:T(8,128)S(1)} %fusion.20), kind=kOutput, calls=%fused_computation.20 | convolution fusion | flops 3225157376 | bytes 5248000 | tf_op jit(solution)/shard_map/dot_general | solution.py:29
  241.9 0.1 multiply_convert_fusion
  242.0 0.5 fusion.34
  242.5 5.8 %fusion.2 = bf16[4096,256]{0,1:T(8,128)(2,1)S(1)} fusion(bf16[1024,256]{0,1:T(8,128)(2,1)S(1)} %multiply_convert_fusion, bf16[4096,1024]{1,0:T(8,128)(2,1)} %param.4, bf16[4096,256]{0,1:T(8,128)(2,1)S(1)} %copy-done.3, f32[256]{0:T(256)S(1)} %bitcast.90), kind=kOutput, calls=%fused_computation.7 | convolution fusion | flops 2151677952 | bytes 13108224 | tf_op jit(solution)/shard_map/dot_general | solution.py:43
  248.3 2.7 copy.21
  251.0 20.9 %scatter_custom_fusion = bf16[8192,256]{1,0:T(8,128)(2,1)} fusion(s32[4096]{0:T(1024)S(1)} %bitcast.89, bf16[4096,256]{1,0:T(8,128)(2,1)} %copy.21, bf16[]{:T(256)} %constant.88.clone.1), kind=kCustom, calls=%fused_computation.17 | custom fusion | bytes 4194816 | tf_op jit(solution)/shard_map/scatter | solution.py:48
  272.0 95.5 %all_to_all.15 = bf16[64,1,128,256]{3,2,1,0:T(8,128)(2,1)S(1)} all-to-all(bf16[64,1,128,256]{3,2,1,0:T(8,128)(2,1)} %bitcast.80), channel_id=1, replica_groups=mesh['dp'=4,'owner'=8] {'owner'}, dimensions={0} | all-to-all | bytes 8388608 | tf_op jit(solution)/shard_map/all_to_all | solution.py:51
  367.5 2.3 copy.23
  (17 shorter events, 0.2 us)
Async XLA Ops:
  6.5 160.6 %copy-start = (f32[1024,256]{1,0:T(8,128)S(1)}, f32[1024,256]{1,0:T(8,128)}, u32[]{:S(2)}) copy-start(f32[1024,256]{1,0:T(8,128)} %param.7) | copy-start | bytes 3145732
  6.5 160.6 %all-reduce.3.cloned.1.call-start = ((), (), s32[]{:S(2)}) async-start(), calls=%async_computation.1 | async-start | bytes 8388608 | tf_op jit(solution)/shard_map/psum | solution.py:20
  21.6 1.6 copy-start.2
  21.6 4.5 %copy-start.4 = (s32[4096,1]{0,1:T(1,128)S(1)}, s32[4096,1]{0,1:T(1,128)}, u32[]{:S(2)}) copy-start(s32[4096,1]{0,1:T(1,128)} %param.5) | copy-start | bytes 49156
  234.9 2.4 copy-start.1
  237.4 5.1 %copy-start.3 = (bf16[4096,256]{0,1:T(8,128)(2,1)S(1)}, bf16[4096,256]{0,1:T(8,128)(2,1)}, u32[]{:S(2)}) copy-start(bf16[4096,256]{0,1:T(8,128)(2,1)} %copy.20) | copy-start | bytes 6291460
Sparse Core Ops, SparseCore 0:
  21.8 145.2 all-reduce.2
where the time goes:
time: 385 us; the launch traced here: 377 us
  blocking collectives  138 us (36%)
  other arithmetic  78.7 us (20%)
  waiting for transfers between devices  73.2 us (19%)
  matrix products  36.5 us (9%)
  local copies, waits for them, and re-layouts  35.3 us (9%)
  between operations  15.3 us (4%)
    all_to_all x1, blocking collectives, shards(): lax.all_to_all(packed, 'owner', split_axis=0, concat_axis=1, tiled=True)  95.5 us
    psum x1, waiting for transfers between devices, shards(): second_all, column_all = lax.psum((second, column_sum), ('dp', 'owner'))  73.1 us
    psum x1, blocking collectives, shards(): second_all, column_all = lax.psum((second, column_sum), ('dp', 'owner'))  42.3 us
    another operation x6, other arithmetic, shards(): lower_factor = jnp.linalg.cholesky(gram_matrix)  34 us
    scatter x1, local copies, waits for them, and re-layouts, shards(): jnp.zeros((clusters * capacity, rank_count), jnp.bfloat16).at[destination]  20.9 us
    another operation x3, other arithmetic, shards(): lax.linalg.triangular_solve(lower_factor, image_rows, left_side=False, lo...  19.7 us
    another operation x3, other arithmetic  19 us
    dot_general x1, matrix products, shards(): lax.dot_general(embeddings, embeddings, (((0,), (0,)), ((), ())), preferr...  15.1 us
  transfers between devices with their start and end apart: 1, of which 1 were waited for; matrix products, arithmetic and copies ran while one was open for 8% of the time, Pallas kernels for 0%

commit v1 on v0

--- a/solution.py
+++ b/solution.py
@@ -17,7 +17,7 @@
     second = lax.dot_general(
         embeddings, embeddings, (((0,), (0,)), ((), ())), preferred_element_type=jnp.float32
     )
-    second_all, column_all = lax.psum((second, column_sum), ("dp", "owner"))
+    second_all, column_all = lax.psum(lax.psum((second, column_sum), "owner"), "dp")
     mean_vec = column_all / row_total
     covariance = second_all / row_total - jnp.outer(mean_vec, mean_vec)
     image_rows = jnp.dot(covariance, start_basis, precision=highest)

time: 385 us -> 488 us (1.27)
  waiting for transfers between devices: 73.2 us -> 191 us
  blocking collectives: 138 us -> 124 us
    psum x1 -> x2, waiting for transfers between devices: 73.1 us -> 191 us  [the longest x1 135 us: shards(): lax.psum((second, column_sum), 'owner')]
    psum x1 -> x2, blocking collectives: 42.3 us -> 25.6 us  [the longest x1 19.1 us: shards(): lax.psum((second, column_sum), 'owner')]
  transfers between devices with their start and end apart: 1 -> 2, of which waited for: 1 -> 2; matrix products, arithmetic and copies ran while one was open for 8% -> 6% of each run, Pallas kernels for 0% -> 0%
where the time goes in v1:
time: 488 us; the launch traced here: 481 us
  waiting for transfers between devices  191 us (39%)
  blocking collectives  124 us (25%)
  other arithmetic  78.6 us (16%)
  matrix products  36.5 us (7%)
  local copies, waits for them, and re-layouts  35.2 us (7%)
  between operations  15.3 us (3%)
    psum x1, waiting for transfers between devices, shards(): lax.psum((second, column_sum), 'owner')  135 us
    all_to_all x1, blocking collectives, shards(): lax.all_to_all(packed, 'owner', split_axis=0, concat_axis=1, tiled=True)  98.6 us
    psum x1, waiting for transfers between devices, shards(): lax.psum(lax.psum((second, column_sum), 'owner'), 'dp')  55.5 us
    another operation x6, other arithmetic, shards(): lower_factor = jnp.linalg.cholesky(gram_matrix)  34 us
    scatter x1, local copies, waits for them, and re-layouts, shards(): jnp.zeros((clusters * capacity, rank_count), jnp.bfloat16).at[destination]  20.9 us
    another operation x3, other arithmetic, shards(): lax.linalg.triangular_solve(lower_factor, image_rows, left_side=False, lo...  19.7 us
    psum x1, blocking collectives, shards(): lax.psum((second, column_sum), 'owner')  19.1 us
    another operation x3, other arithmetic  19 us
  transfers between devices with their start and end apart: 2, of which 2 were waited for; matrix products, arithmetic and copies ran while one was open for 6% of the time, Pallas kernels for 0%

profile of v1, /device:TPU:0, one launch (start us, length us, event | category | flops | bytes accessed | tf_op | source)
XLA Modules:
  0.0 480.8 jit_solution(8025829607703992178)
XLA Ops:
  6.5 0.0 copy-start
  6.5 15.1 %fusion.32 = f32[1024,1024]{1,0:T(8,128)} fusion(bf16[4096,1024]{1,0:T(8,128)(2,1)} %param.4), kind=kOutput, calls=%fused_computation.64 | convolution fusion | flops 8589934592 | bytes 12582912 | tf_op jit(solution)/shard_map/dot_general | solution.py:17
  21.6 0.0 all-reduce.4.cloned.1.call-update
  21.7 0.0 all-reduce.6.cloned.1.call-start
  21.7 1.5 copy-done.2
  23.2 2.9 copy.20
  26.1 0.1 fusion.18
  26.3 18.4 %reduce-window.6 = s32[64,32,128]{2,1,0:T(8,128)S(1)} reduce-window(s32[64,32,128]{2,1,0:T(8,128)S(1)} %fusion.18, s32[]{:T(128)} %copy.39), window={size=1x1x128 pad=0_0x0_0x127_0}, to_apply=%region_0.0 | reduce-window | flops 33292288 | bytes 2097156 | tf_op jit(solution)/shard_map/reduce-window
  44.7 0.3 slice.61
  45.0 0.4 copy.25
  45.5 0.2 reduce-window.9
  45.7 135.4 %all-reduce.4.cloned.1.call-done = f32[1024,1024]{1,0:T(8,128)} async-done(((f32[1024,1024]{1,0:T(8,128)}), f32[1024,1024]{1,0:T(8,128)}) %all-reduce.4.cloned.1.call-update) | async-done | bytes 4194320 | tf_op jit(solution)/shard_map/psum | solution.py:20
  181.1 0.0 all-reduce.6.cloned.1.call-update
  181.1 4.6 convert_reduce_fusion
  185.7 19.1 %psum.30 = f32[1024]{0:T(1024)S(1)} all-reduce(f32[1024]{0:T(1024)S(1)} %convert_reduce_fusion), channel_id=1, replica_groups=mesh['dp'=4,'owner'=8] {'owner'}, use_global_device_ids=true, to_apply=%region_6.7 | all-reduce | flops 1024 | bytes 8192 | tf_op jit(solution)/shard_map/psum | solution.py:20
  204.8 6.5 %psum.31 = f32[1024]{0:T(1024)S(1)} all-reduce(f32[1024]{0:T(1024)S(1)} %psum.30), channel_id=1, replica_groups=mesh['dp'=4,'owner'=8] {'dp'}, use_global_device_ids=true, to_apply=%region_7.8 | all-reduce | flops 1024 | bytes 8192 | tf_op jit(solution)/shard_map/psum | solution.py:20
  211.3 0.3 broadcast_add_fusion
  211.7 0.9 fusion.17
  212.6 55.5 %all-reduce.6.cloned.1.call-done = f32[1024,1024]{1,0:T(8,128)} async-done(((f32[1024,1024]{1,0:T(8,128)}), f32[1024,1024]{1,0:T(8,128)}) %all-reduce.6.cloned.1.call-update) | async-done | bytes 4194320 | tf_op jit(solution)/shard_map/psum | solution.py:20
  268.1 6.1 %fusion.4 = f32[1024,256]{1,0:T(8,128)S(1)} fusion(f32[1024,256]{1,0:T(8,128)S(1)} %copy-done, f32[1024,1024]{1,0:T(8,128)} %all-reduce.6.cloned.1.call-done, f32[1024]{0:T(1024)S(1)} %broadcast_multiply_fusion), kind=kOutput, calls=%fused_computation.10 | convolution fusion | flops 3224371200 | bytes 6295552 | tf_op jit(solution)/shard_map/dot_general | solution.py:23
  274.1 1.8 fusion.33
  276.0 0.1 copy.18
  276.2 11.7 %cholesky.50 = f32[128,128]{1,0:T(8,128)S(1)} custom-call(f32[128,128]{1,0:T(8,128)S(1)} %cholesky.118), custom_call_target="Cholesky" | custom-call | tf_op jit(solution)/shard_map/jit(cholesky)/cholesky | solution.py:25
  287.9 9.8 %custom-call.14 = f32[1,128,128]{1,2,0:T(8,128)S(1)} custom-call(f32[1,128,128]{2,1,0:T(8,128)S(1)} %get-tuple-element.26), custom_call_target="InvertDiagBlocksLowerTriangular" | custom-call | tf_op jit(solution)/shard_map/jit(cholesky)/cholesky | solution.py:25
  297.8 0.2 constant_dynamic-update-slice_fusion.1
  298.0 0.3 convolution_subtract_fusion.2
  298.3 11.7 %cholesky.105 = f32[128,128]{1,0:T(8,128)S(1)} custom-call(f32[128,128]{1,0:T(8,128)S(1)} %convolution_subtract_fusion.2), custom_call_target="Cholesky" | custom-call | tf_op jit(solution)/shard_map/jit(cholesky)/cholesky | solution.py:25
  310.0 0.7 compare_reduce_fusion
  312.1 0.1 triangular_solve.58
  312.2 3.9 while.1
  312.2 0.6 fusion.49
  312.8 1.4 bitcast_dynamic-update-slice_fusion.2
  314.2 0.6 fusion.49
  314.8 1.4 bitcast_dynamic-update-slice_fusion.2
  316.1 19.7 %custom-call.15 = f32[2,128,128]{1,2,0:T(8,128)S(1)} custom-call(f32[2,128,128]{2,1,0:T(8,128)S(1)} %get-tuple-element.12), custom_call_target="InvertDiagBlocksLowerTriangular" | custom-call | tf_op jit(solution)/shard_map/triangular_solve | solution.py:26
  335.8 0.6 fusion.20
  336.5 1.0 convolution_subtract_fusion.1
  337.5 0.6 fusion.23
  338.1 0.2 fusion.19
  338.3 4.5 fusion.14
  342.8 0.1 multiply_convert_fusion
  342.9 0.5 fusion.34
  343.4 0.0 copy-done.3
  343.4 5.8 %fusion.2 = bf16[4096,256]{0,1:T(8,128)(2,1)S(1)} fusion(bf16[1024,256]{0,1:T(8,128)(2,1)S(1)} %multiply_convert_fusion, bf16[4096,1024]{1,0:T(8,128)(2,1)} %param.4, bf16[4096,256]{0,1:T(8,128)(2,1)S(1)} %copy-done.3, f32[256]{0:T(256)S(1)} %bitcast.90), kind=kOutput, calls=%fused_computation.7 | convolution fusion | flops 2151677952 | bytes 13108224 | tf_op jit(solution)/shard_map/dot_general | solution.py:43
  349.2 2.7 copy.21
  351.9 20.9 %scatter_custom_fusion = bf16[8192,256]{1,0:T(8,128)(2,1)} fusion(s32[4096]{0:T(1024)S(1)} %bitcast.89, bf16[4096,256]{1,0:T(8,128)(2,1)} %copy.21, bf16[]{:T(256)} %constant.88.clone.1), kind=kCustom, calls=%fused_computation.17 | custom fusion | bytes 4194816 | tf_op jit(solution)/shard_map/scatter | solution.py:48
  372.8 98.6 %all_to_all.15 = bf16[64,1,128,256]{3,2,1,0:T(8,128)(2,1)S(1)} all-to-all(bf16[64,1,128,256]{3,2,1,0:T(8,128)(2,1)} %bitcast.80), channel_id=1, replica_groups=mesh['dp'=4,'owner'=8] {'owner'}, dimensions={0} | all-to-all | bytes 8388608 | tf_op jit(solution)/shard_map/all_to_all | solution.py:51
  471.4 2.3 copy.23
  (21 shorter events, 0.2 us)
Async XLA Ops:
  6.5 261.5 %copy-start = (f32[1024,256]{1,0:T(8,128)S(1)}, f32[1024,256]{1,0:T(8,128)}, u32[]{:S(2)}) copy-start(f32[1024,256]{1,0:T(8,128)} %param.7) | copy-start | bytes 3145732
  6.5 174.5 %all-reduce.4.cloned.1.call-start = ((), (), s32[]{:S(2)}) async-start(), calls=%async_computation.1 | async-start | bytes 8388608 | tf_op jit(solution)/shard_map/psum | solution.py:20
  21.6 1.6 copy-start.2
  21.6 4.5 copy-start.4
  21.7 246.4 %all-reduce.6.cloned.1.call-start = ((), (), s32[]{:S(2)}) async-start(), calls=%async_computation.2 | async-start | bytes 8388608 | tf_op jit(solution)/shard_map/psum | solution.py:20
  335.8 2.4 copy-start.1
  338.3 5.1 %copy-start.3 = (bf16[4096,256]{0,1:T(8,128)(2,1)S(1)}, bf16[4096,256]{0,1:T(8,128)(2,1)}, u32[]{:S(2)}) copy-start(bf16[4096,256]{0,1:T(8,128)(2,1)} %copy.20) | copy-start | bytes 6291460
Sparse Core Ops, SparseCore 0:
  21.8 159.2 all-reduce.3
  183.4 84.5 all-reduce.5
